TPU v7x, 32 devices: a whole 2x2x4 slice. The times are simulated.
32 devices in a mesh: rows: 8 (over z, y), vecs: 4 (over x, core).
Axes of the slice: x: 2, y: 2, z: 4, core: 2. Of those that a mesh axis runs over, the one named last changes fastest.
Arguments:
- vectors: bfloat16 [32768, 1024], P('rows', 'vecs'), may hold values from -6 to 6, as said below
- blocks: bfloat16 [256, 5, 128, 128], P('rows'), may hold values from -0.25 to 0.25
- columns: int32 [256, 5], P('rows'), may hold values from 0 to 255, as said below
Outputs:
- basis: float32 [32768, 1024], P('rows', 'vecs')
Inputs may be any that keep to these rules, and one draw needn't show every extreme that they name: Each block row i names 5 block columns of the form i + d clipped to 0 .. 255, with distinct d in -8 .. 8; near the grid's ends some may repeat. `vectors`: entries of order one.
All inputs are finite; a program needn't handle non-finite values.
Results may differ from a plain program's by a relative error of at most 0.0075.
Values may be sent and summed in bfloat16 or wider, within the bound.
A program may use at most 128 MiB of HBM per device.

v0:
```python
import functools

import jax
import jax.numpy as jnp
from jax import lax
from jax.experimental import pallas as pl
from jax.experimental.pallas import tpu as pltpu
from jax.sharding import PartitionSpec as P

DEGREE = 4

filter_center = 0.25
filter_radius = 1.25

HIGHEST = lax.Precision.HIGHEST
VMEM_LIMIT = 56 * 1024 * 1024
PIVOTS = 8


def step_kernel(group, n_pieces, kind, emit_f32, index_ref, *refs):
    pieces = refs[:n_pieces]
    blocks_ref = refs[n_pieces]
    rest = refs[n_pieces + 1 :]
    if kind == "first":
        (cur_ref, *outs), old_ref = rest, None
    else:
        cur_ref, old_ref, *outs = rest
    *outs, window = outs
    step = pl.program_id(0)
    size_b = blocks_ref.shape[2]
    nnz = blocks_ref.shape[1]

    @pl.when(step == 0)
    def _():
        start = 0
        for piece in pieces:
            count = piece.shape[0]
            window[start : start + count, :] = piece[...]
            start += count

    for g in range(group):
        acc = None
        for j in range(nnz):
            at = pl.multiple_of(index_ref[(step * group + g) * nnz + j] * size_b, size_b)
            part = jnp.dot(
                blocks_ref[g, j], window[pl.ds(at, size_b), :], preferred_element_type=jnp.float32
            )
            acc = part if acc is None else acc + part
        rows = slice(g * size_b, (g + 1) * size_b)
        cur = cur_ref[rows, :].astype(jnp.float32)
        new = (acc - filter_center * cur) * (1.0 / filter_radius)
        if kind != "first":
            new = 2.0 * new - old_ref[rows, :].astype(jnp.float32)
        outs[0][rows, :] = new.astype(jnp.bfloat16)
        if emit_f32:
            outs[1][rows, :] = new


def chebyshev_step(index, pieces, blocks, row_of, count, cur, old, kind, emit_f32):
    size_b, nnz = blocks.shape[2], blocks.shape[1]
    width = pieces[0].shape[1]
    group = 4 if count % 4 == 0 else 1
    whole = lambda i, ix: (0, 0)
    part = lambda i, ix: (i, 0)
    tall = (group * size_b, width)
    in_specs = [pl.BlockSpec(p.shape, whole) for p in pieces]
    in_specs.append(
        pl.BlockSpec((group, nnz, size_b, size_b), lambda i, ix: (row_of(i, group), 0, 0, 0))
    )
    operands = list(pieces) + [blocks, cur]
    in_specs.append(pl.BlockSpec(tall, part))
    if kind != "first":
        operands.append(old)
        in_specs.append(pl.BlockSpec(tall, part))
    rows = count * size_b
    out_shape = [jax.ShapeDtypeStruct((rows, width), jnp.bfloat16)]
    if emit_f32:
        out_shape.append(jax.ShapeDtypeStruct((rows, width), jnp.float32))
    window_rows = sum(p.shape[0] for p in pieces)
    return pl.pallas_call(
        functools.partial(step_kernel, group, len(pieces), kind, emit_f32),
        grid_spec=pltpu.PrefetchScalarGridSpec(
            num_scalar_prefetch=1,
            grid=(count // group,),
            in_specs=in_specs,
            out_specs=[pl.BlockSpec(tall, part) for _ in out_shape],
            scratch_shapes=[pltpu.VMEM((window_rows, width), jnp.bfloat16)],
        ),
        out_shape=out_shape,
        compiler_params=pltpu.CompilerParams(vmem_limit_bytes=VMEM_LIMIT),
        cost_estimate=pl.CostEstimate(
            flops=2 * rows * nnz * size_b * width,
            bytes_accessed=rows * nnz * size_b * 2 + rows * width * 16,
            transcendentals=0,
        ),
    )(index, *operands)


def factor_block(block):
    size = block.shape[0]
    tiles = [block[8 * t : 8 * (t + 1), :] for t in range(size // 8)]
    lane = lax.broadcasted_iota(jnp.int32, (8, size), 1)
    sub = lax.broadcasted_iota(jnp.int32, (8, size), 0)

    def spread(array):
        return jnp.broadcast_to(array, (8, size))

    for j in range(0, size, PIVOTS):
        first, r = divmod(j, 8)
        each = range(PIVOTS)
        at_any = jnp.logical_and(lane >= j, lane < j + PIVOTS)
        head = tiles[first]
        cols = [spread(head[:, j + a : j + a + 1]) for a in each]
        pivots = [[spread(cols[a][r + b : r + b + 1, :]) for a in range(b + 1)] for b in each]
        rows = [jnp.where(at_any, 0.0, spread(head[r + a : r + a + 1, :])) for a in each]
        rows = [jnp.where(lane == j + a, 1.0, rows[a]) for a in each]
        over, ratio = [], {}
        for a in each:
            over.append(1.0 / pivots[a][a])
            for b in range(a + 1, PIVOTS):
                ratio[b, a] = pivots[b][a] * over[a]
                for c in range(a + 1, b + 1):
                    pivots[b][c] = pivots[b][c] - ratio[b, a] * pivots[c][a]
                rows[b] = rows[b] - ratio[b, a] * rows[a]
        use = [None] * PIVOTS
        for a in reversed(each):
            use[a] = rows[a] * over[a]
            for b in range(a + 1, PIVOTS):
                use[a] = use[a] - ratio[b, a] * use[b]
        start = first if r + PIVOTS < 8 else first + 1
        for t in range(start, size // 8):
            tile = tiles[t]
            if t > first:
                cols = [spread(tile[:, j + a : j + a + 1]) for a in each]
            terms = [cols[a] * use[a] for a in each]
            while len(terms) > 1:
                terms = [x + y for x, y in zip(terms[::2], terms[1::2])]
            tiles[t] = jnp.where(at_any, 0.0, tile) - terms[0]
        top = jnp.where(sub < r, head, tiles[first])
        for a in each:
            top = jnp.where(sub == r + a, rows[a] * lax.rsqrt(pivots[a][a]), top)
        tiles[first] = top
    return jnp.concatenate(tiles, axis=0)


def inverse_kernel(size, total_rows, panels, gram_ref, out_ref, work, factor):
    full = gram_ref.shape[0]
    count = full // size
    wide = full // panels
    half = panels // 2
    work[...] = jnp.zeros_like(work)
    for low in range(panels):
        for high in range(low, panels):
            apart = high - low
            own, other = slice(low * wide, (low + 1) * wide), slice(high * wide, (high + 1) * wide)
            if not shared(panels, wide):
                work[own, other] = gram_ref[own, other] / total_rows
            elif apart < half:
                work[own, other] = gram_ref[own, apart * wide : (apart + 1) * wide] / total_rows
            elif apart > half:
                back = panels - apart
                part = gram_ref[other, back * wide : (back + 1) * wide] / total_rows
                work[own, other] = part.T
            else:
                middle = high * wide + wide // 2
                last = slice(half * wide, half * wide + wide // 2)
                work[own, high * wide : middle] = gram_ref[own, last] / total_rows
                work[own, middle : (high + 1) * wide] = gram_ref[other, last] / total_rows

    @pl.loop(0, count)
    def _(k):
        at = pl.multiple_of(k * size, size)
        done = factor_block(work[pl.ds(at, size), pl.ds(at, size)])
        down = lax.broadcasted_iota(jnp.int32, (size, size), 0)
        across = lax.broadcasted_iota(jnp.int32, (size, size), 1)
        factor[...] = jnp.where(across <= down, done, 0.0)
        for c in range(count):
            own = slice(c * size, (c + 1) * size)
            below = slice((c + 1) * size, full)

            @pl.when(k == c)
            def _():
                lower_inv = factor[...]
                left = slice(0, c * size)
                if c > 0:
                    out_ref[own, left] = jnp.dot(
                        lower_inv, work[own, left], precision=HIGHEST,
                        preferred_element_type=jnp.float32,
                    )
                out_ref[own, own] = lower_inv
                if c + 1 < count:
                    out_ref[own, below] = jnp.zeros((size, full - (c + 1) * size), jnp.float32)
                    right = jnp.dot(
                        lower_inv, work[own, below], precision=HIGHEST,
                        preferred_element_type=jnp.float32,
                    )
                    down_left = (((0,), (0,)), ((), ()))
                    work[below, below] -= lax.dot_general(
                        right, right, down_left, precision=HIGHEST,
                        preferred_element_type=jnp.float32,
                    )
                    known = slice(0, (c + 1) * size)
                    change = lax.dot_general(
                        right, out_ref[own, known], down_left, precision=HIGHEST,
                        preferred_element_type=jnp.float32,
                    )
                    if c > 0:
                        work[below, left] -= change[:, : c * size]
                    work[below, own] = -change[:, c * size :]


def shared(panels, wide):
    return panels % 2 == 0 and wide % 256 == 0


def panel_part(panel):
    panels, wide = lax.axis_size("vecs"), panel.shape[0]
    if not shared(panels, wide):
        return panel
    me, half, short = lax.axis_index("vecs"), panels // 2, wide // 2
    twice = jnp.concatenate([panel, panel], axis=1)
    near = lax.dynamic_slice_in_dim(twice, me * wide, half * wide, 1)
    far = lax.dynamic_slice_in_dim(twice, (me + half) * wide, wide, 1)
    middle = jnp.where(me < half, far[:, :short], far[short:, :].T)
    return jnp.concatenate([near, middle], axis=1)


def inverse_factor(gram, total_rows, panels):
    full = gram.shape[0]
    size = 128
    return pl.pallas_call(
        functools.partial(inverse_kernel, size, total_rows, panels),
        out_shape=jax.ShapeDtypeStruct((full, full), jnp.float32),
        in_specs=[pl.BlockSpec(memory_space=pltpu.VMEM)],
        out_specs=pl.BlockSpec(memory_space=pltpu.VMEM),
        scratch_shapes=[
            pltpu.VMEM((full, full), jnp.float32),
            pltpu.VMEM((size, size), jnp.float32),
        ],
        compiler_params=pltpu.CompilerParams(vmem_limit_bytes=VMEM_LIMIT),
        cost_estimate=pl.CostEstimate(
            flops=40 * full * full * full, bytes_accessed=8 * full * full, transcendentals=full
        ),
    )(gram)


def split_apply(left_bf, factor):
    factor_high = factor.astype(jnp.bfloat16)
    factor_low = (factor - factor_high.astype(jnp.float32)).astype(jnp.bfloat16)
    first = jnp.dot(left_bf, factor_high.T, preferred_element_type=jnp.float32)
    second = jnp.dot(left_bf, factor_low.T, preferred_element_type=jnp.float32)
    return first + second


def filtered_block(vectors, blocks, columns):
    block_rows, nnz, size_b = blocks.shape[:3]
    reach = block_rows // 4
    edge = reach * size_b
    first_row = lax.axis_index("rows") * block_rows
    local = columns - first_row
    edges_index = jnp.concatenate([local[:reach], local[block_rows - reach :]], axis=0) + reach
    edges_index = edges_index.reshape(-1)
    inner_index = local[reach : block_rows - reach].reshape(-1)
    inner_rows = block_rows - 2 * reach

    axis_size = lax.axis_size("rows")
    up = [(i, i + 1) for i in range(axis_size - 1)]
    down = [(j, i) for i, j in up]

    def inner_of(i, group):
        return i + reach // group

    def edges_of(i, group):
        return jnp.where(i < reach // group, i, i + inner_rows // group)

    def halves(array):
        return jnp.concatenate([array[:edge], array[-edge:]], axis=0), array[edge:-edge]

    cur_edges, cur_inner = halves(vectors)
    bf_edges, bf_inner = cur_edges, cur_inner
    old_edges = old_inner = None
    for iteration in range(DEGREE):
        kind = "first" if iteration == 0 else "next"
        emit_f32 = iteration < DEGREE - 1
        low, high = bf_edges[:edge], bf_edges[edge:]
        before = lax.ppermute(high, "rows", up)
        after = lax.ppermute(low, "rows", down)
        own = [low, bf_inner, high]
        new_inner = chebyshev_step(
            inner_index, own, blocks, inner_of, inner_rows, cur_inner, old_inner, kind, emit_f32
        )
        new_edges = chebyshev_step(
            edges_index, [before] + own + [after], blocks, edges_of, 2 * reach,
            cur_edges, old_edges, kind, emit_f32,
        )
        old_edges, old_inner = cur_edges, cur_inner
        bf_edges, bf_inner = new_edges[0], new_inner[0]
        if emit_f32:
            cur_edges, cur_inner = new_edges[1], new_inner[1]
    return jnp.concatenate([bf_edges[:edge], bf_inner, bf_edges[edge:]], axis=0)


def shards(vectors, blocks, columns):
    total_rows = vectors.shape[0] * lax.axis_size("rows")
    final = filtered_block(vectors, blocks, columns)
    panel_width = final.shape[1]
    whole_block = lax.all_gather(final, "vecs", axis=1, tiled=True)
    panel = lax.dot_general(
        final, whole_block, (((0,), (0,)), ((), ())), preferred_element_type=jnp.float32
    )
    summed = lax.psum(panel_part(panel), "rows")
    gram = lax.all_gather(summed, "vecs", axis=0, tiled=True)
    inverse = inverse_factor(gram, total_rows, lax.axis_size("vecs"))
    own_rows = lax.dynamic_slice_in_dim(
        inverse, lax.axis_index("vecs") * panel_width, panel_width, 0
    )
    return split_apply(whole_block, own_rows)


def solution(mesh):
    in_specs = (P("rows", "vecs"), P("rows", None, None, None), P("rows", None))
    out_specs = P("rows", "vecs")
    return jax.shard_map(shards, mesh=mesh, in_specs=in_specs, out_specs=out_specs, check_vma=False)
```

profile of v0, /device:TPU:3, one launch (start us, length us, event | category | flops | bytes accessed | tf_op | source)
XLA Modules:
  0.0 413.1 jit_solution(16204966987759582352)
XLA Ops:
  9.1 4.0 collective-permute-start
  17.4 5.2 %collective-permute-done.1.refs_4_ = bf16[1024,256]{1,0:T(8,128)(2,1)S(1)} collective-permute-done((bf16[1024,256]{1,0:T(8,128)(2,1)S(1)}, bf16[1024,256]{1,0:T(8,128)(2,1)S(1)}, u32[]{:S(2)}, u32[]{:S(2)}) %collective-permute-start.1) | collective-permute-done | bytes 524320 | tf_op jit(solution)/shard_map/ppermute | solution.py:287
  22.5 12.2 %collective-permute-done.refs_0_ = bf16[1024,256]{1,0:T(8,128)(2,1)S(1)} collective-permute-done((bf16[1024,256]{1,0:T(8,128)(2,1)S(1)}, bf16[1024,256]{1,0:T(8,128)(2,1)S(1)}, u32[]{:S(2)}, u32[]{:S(2)}) %collective-permute-start) | collective-permute-done | bytes 524320 | tf_op jit(solution)/shard_map/ppermute | solution.py:286
  35.6 7.0 %shard_map.37 = (bf16[2048,256]{1,0:T(8,128)(2,1)}, f32[2048,256]{1,0:T(8,128)}) custom-call(s32[80]{0:T(128)} %add.29.index_ref, bf16[1024,256]{1,0:T(8,128)(2,1)} %copy-done.10, bf16[1024,256]{1,0:T(8,128)(2,1)} %copy-done, bf16[2048,256]{1,0:T(8,128)(2,1)} %slice.52.refs_2_.refs_1_.refs_4_.refs_5_, bf16[1024,256]{1,0:T(8,128)(2,1)} %copy-done.1, ...), custom_call_target="tpu_custom_call" | custom-call | flops 671088640 | bytes 11010048 | tf_op jit(solution)/shard_map/pallas_call | solution.py:80
  45.2 4.8 %collective-permute-start.2 = (bf16[1024,256]{1,0:T(8,128)(2,1)S(1)}, bf16[1024,256]{1,0:T(8,128)(2,1)S(1)}, u32[]{:S(2)}, u32[]{:S(2)}) collective-permute-start(bf16[1024,256]{1,0:T(8,128)(2,1)S(1)} %get-tuple-element.38.refs_3_.refs_2_), channel_id=1, source_target_pairs={{0,4},{4,8},{8,12},{12,16},{16,20},{20,24},{24,28},{1,5},{5,9},{9,... | collective-permute-start | bytes 1572872 | tf_op jit(solution)/shard_map/ppermute | solution.py:286
  50.8 6.9 %shard_map.38 = (bf16[2048,256]{1,0:T(8,128)(2,1)}, f32[2048,256]{1,0:T(8,128)}) custom-call(s32[80]{0:T(128)} %reshape.7.index_ref, bf16[1024,256]{1,0:T(8,128)(2,1)} %copy-done, bf16[2048,256]{1,0:T(8,128)(2,1)} %slice.52.refs_2_.refs_1_.refs_4_.refs_5_, bf16[1024,256]{1,0:T(8,128)(2,1)} %copy-done.1, bf16[32,5,128,128]{3,2,1,0:T(8,128)(2,1)} %refs_3_.7, ...), custom_call_target="tpu_custom_call" | custom-call | flops 671088640 | bytes 11010048 | tf_op jit(solution)/shard_map/pallas_call | solution.py:80
  59.8 11.9 %collective-permute-done.2.refs_0_ = bf16[1024,256]{1,0:T(8,128)(2,1)S(1)} collective-permute-done((bf16[1024,256]{1,0:T(8,128)(2,1)S(1)}, bf16[1024,256]{1,0:T(8,128)(2,1)S(1)}, u32[]{:S(2)}, u32[]{:S(2)}) %collective-permute-start.2) | collective-permute-done | bytes 524320 | tf_op jit(solution)/shard_map/ppermute | solution.py:286
  72.6 7.7 %shard_map.39 = (bf16[2048,256]{1,0:T(8,128)(2,1)}, f32[2048,256]{1,0:T(8,128)}) custom-call(s32[80]{0:T(128)} %add.29.index_ref, bf16[1024,256]{1,0:T(8,128)(2,1)} %copy-done.13, bf16[1024,256]{1,0:T(8,128)(2,1)} %copy-done.4, bf16[2048,256]{1,0:T(8,128)(2,1)} %get-tuple-element.18.refs_2_.refs_1_, bf16[1024,256]{1,0:T(8,128)(2,1)} %copy-done.5, ...), custom_call_target="tpu_custom_call" | custom-call | flops 671088640 | bytes 11010048 | tf_op jit(solution)/shard_map/pallas_call | solution.py:80
  82.9 4.8 %collective-permute-start.4 = (bf16[1024,256]{1,0:T(8,128)(2,1)S(1)}, bf16[1024,256]{1,0:T(8,128)(2,1)S(1)}, u32[]{:S(2)}, u32[]{:S(2)}) collective-permute-start(bf16[1024,256]{1,0:T(8,128)(2,1)S(1)} %get-tuple-element.36.refs_3_.refs_2_), channel_id=1, source_target_pairs={{0,4},{4,8},{8,12},{12,16},{16,20},{20,24},{24,28},{1,5},{5,9},{9,... | collective-permute-start | bytes 1572872 | tf_op jit(solution)/shard_map/ppermute | solution.py:286
  87.6 7.4 %shard_map.40 = (bf16[2048,256]{1,0:T(8,128)(2,1)}, f32[2048,256]{1,0:T(8,128)}) custom-call(s32[80]{0:T(128)} %reshape.7.index_ref, bf16[1024,256]{1,0:T(8,128)(2,1)} %copy-done.4, bf16[2048,256]{1,0:T(8,128)(2,1)} %get-tuple-element.18.refs_2_.refs_1_, bf16[1024,256]{1,0:T(8,128)(2,1)} %copy-done.5, bf16[32,5,128,128]{3,2,1,0:T(8,128)(2,1)} %refs_3_.7, ...), custom_call_target="tpu_custom_call" | custom-call | flops 671088640 | bytes 11010048 | tf_op jit(solution)/shard_map/pallas_call | solution.py:80
  97.5 11.9 %collective-permute-done.4.refs_0_ = bf16[1024,256]{1,0:T(8,128)(2,1)S(1)} collective-permute-done((bf16[1024,256]{1,0:T(8,128)(2,1)S(1)}, bf16[1024,256]{1,0:T(8,128)(2,1)S(1)}, u32[]{:S(2)}, u32[]{:S(2)}) %collective-permute-start.4) | collective-permute-done | bytes 524320 | tf_op jit(solution)/shard_map/ppermute | solution.py:286
  110.3 8.0 %shard_map.41 = (bf16[2048,256]{1,0:T(8,128)(2,1)}, f32[2048,256]{1,0:T(8,128)}) custom-call(s32[80]{0:T(128)} %add.29.index_ref, bf16[1024,256]{1,0:T(8,128)(2,1)} %copy-done.14, bf16[1024,256]{1,0:T(8,128)(2,1)} %copy-done.2, bf16[2048,256]{1,0:T(8,128)(2,1)} %get-tuple-element.22.refs_2_.refs_1_, bf16[1024,256]{1,0:T(8,128)(2,1)} %copy-done.3, ...), custom_call_target="tpu_custom_call" | custom-call | flops 671088640 | bytes 11010048 | tf_op jit(solution)/shard_map/pallas_call | solution.py:80
  120.8 4.8 %collective-permute-start.6 = (bf16[1024,256]{1,0:T(8,128)(2,1)S(1)}, bf16[1024,256]{1,0:T(8,128)(2,1)S(1)}, u32[]{:S(2)}, u32[]{:S(2)}) collective-permute-start(bf16[1024,256]{1,0:T(8,128)(2,1)S(1)} %get-tuple-element.34.refs_3_.refs_2_), channel_id=1, source_target_pairs={{0,4},{4,8},{8,12},{12,16},{16,20},{20,24},{24,28},{1,5},{5,9},{9,... | collective-permute-start | bytes 1572872 | tf_op jit(solution)/shard_map/ppermute | solution.py:286
  125.6 7.5 %shard_map.42 = (bf16[2048,256]{1,0:T(8,128)(2,1)}, f32[2048,256]{1,0:T(8,128)}) custom-call(s32[80]{0:T(128)} %reshape.7.index_ref, bf16[1024,256]{1,0:T(8,128)(2,1)} %copy-done.2, bf16[2048,256]{1,0:T(8,128)(2,1)} %get-tuple-element.22.refs_2_.refs_1_, bf16[1024,256]{1,0:T(8,128)(2,1)} %copy-done.3, bf16[32,5,128,128]{3,2,1,0:T(8,128)(2,1)} %refs_3_.7, ...), custom_call_target="tpu_custom_call" | custom-call | flops 671088640 | bytes 11010048 | tf_op jit(solution)/shard_map/pallas_call | solution.py:80
  133.1 7.0 %shard_map.44 = bf16[2048,256]{1,0:T(8,128)(2,1)} custom-call(s32[80]{0:T(128)} %reshape.7.index_ref, bf16[1024,256]{1,0:T(8,128)(2,1)} %copy-done.6, bf16[2048,256]{1,0:T(8,128)(2,1)} %get-tuple-element.26.refs_2_.refs_1_, bf16[1024,256]{1,0:T(8,128)(2,1)} %copy-done.7, bf16[32,5,128,128]{3,2,1,0:T(8,128)(2,1)} %refs_3_.7, ...), custom_call_target="tpu_custom_call" | custom-call | flops 671088640 | bytes 11010048 | tf_op jit(solution)/shard_map/pallas_call | solution.py:80
  140.1 7.2 %collective-permute-done.6.refs_0_ = bf16[1024,256]{1,0:T(8,128)(2,1)S(1)} collective-permute-done((bf16[1024,256]{1,0:T(8,128)(2,1)S(1)}, bf16[1024,256]{1,0:T(8,128)(2,1)S(1)}, u32[]{:S(2)}, u32[]{:S(2)}) %collective-permute-start.6) | collective-permute-done | bytes 524320 | tf_op jit(solution)/shard_map/ppermute | solution.py:286
  148.2 7.5 %shard_map.43 = bf16[2048,256]{1,0:T(8,128)(2,1)} custom-call(s32[80]{0:T(128)} %add.29.index_ref, bf16[1024,256]{1,0:T(8,128)(2,1)} %copy-done.16, bf16[1024,256]{1,0:T(8,128)(2,1)} %copy-done.6, bf16[2048,256]{1,0:T(8,128)(2,1)} %get-tuple-element.26.refs_2_.refs_1_, bf16[1024,256]{1,0:T(8,128)(2,1)} %copy-done.7, bf16[1024,256]{1,0:T(8,128)(2,1)} %copy-done.15, ...), custom_call_target="tpu_custom_call" | custom-call | flops 671088640 | bytes 11010048 | tf_op jit(solution)/shard_map/pallas_call | solution.py:80
  158.5 59.8 %all-gather.3.cloned.1.call-done = bf16[4096,1024]{1,0:T(8,128)(2,1)} async-done(((bf16[4096,256]{1,0:T(8,128)(2,1)}), bf16[4096,1024]{1,0:T(8,128)(2,1)}) %all-gather.3.cloned.1.call-update) | async-done | bytes 8388624 | tf_op jit(solution)/shard_map/all_gather | solution.py:307
  218.2 6.7 %fusion.6 = f32[256,1024]{0,1:T(8,128)S(1)} fusion(bf16[4096,1024]{1,0:T(8,128)(2,1)} %all-gather.3.cloned.1.call-done, bf16[1024,256]{1,0:T(8,128)(2,1)S(1)} %get-tuple-element.32, bf16[2048,256]{1,0:T(8,128)(2,1)S(1)} %copy-done.8, bf16[1024,256]{1,0:T(8,128)(2,1)S(1)} %get-tuple-element.31), kind=kOutput, calls=%fused_computation.19 | convolution fusion | flops 2153775104 | bytes 11534336 | tf_op jit(solution)/shard_map/dot_general | solution.py:308
  226.6 72.9 %all-reduce.2.cloned.1.call-done = f32[256,640]{1,0:T(8,128)} async-done(((f32[256,640]{1,0:T(8,128)}), f32[256,640]{1,0:T(8,128)}) %all-reduce.2.cloned.1.call-update) | async-done | bytes 655376 | tf_op jit(solution)/shard_map/psum | solution.py:311
  299.5 27.1 %all-gather.5.cloned.1.call-done.gram_ref = f32[1024,640]{1,0:T(8,128)} async-done(((f32[256,640]{1,0:T(8,128)}), f32[1024,640]{1,0:T(8,128)}) %all-gather.5.cloned.1.call-update) | async-done | bytes 2621456 | tf_op jit(solution)/shard_map/all_gather | solution.py:312
  326.5 65.6 %shard_map.45 = f32[1024,1024]{1,0:T(8,128)} custom-call(f32[1024,640]{1,0:T(8,128)} %all-gather.5.cloned.1.call-done.gram_ref), custom_call_target="tpu_custom_call" | custom-call | flops 42949672960 | bytes 8388608 | tf_op jit(solution)/shard_map/pallas_call | solution.py:231
  392.2 6.1 %fusion.2 = f32[4096,256]{1,0:T(8,128)S(1)} fusion(bf16[4096,1024]{1,0:T(8,128)(2,1)} %all-gather.3.cloned.1.call-done, f32[1024,1024]{1,0:T(8,128)} %shard_map.45, s32[]{:T(128)S(6)} %select_n.21), kind=kOutput, calls=%fused_computation.12 | convolution fusion | flops 2147483648 | bytes 13107204 | tf_op jit(solution)/shard_map/dot_general | solution.py:250
  398.3 8.3 %convolution_add_fusion = f32[4096,256]{1,0:T(8,128)} fusion(f32[4096,256]{1,0:T(8,128)S(1)} %fusion.2, bf16[4096,1024]{1,0:T(8,128)(2,1)} %all-gather.3.cloned.1.call-done, f32[1024,1024]{1,0:T(8,128)} %shard_map.45, s32[]{:T(128)S(6)} %select_n.21), kind=kOutput, calls=%fused_computation | convolution fusion | flops 2149580800 | bytes 17825796 | tf_op jit(solution)/shard_map/dot_general | solution.py:251
  (72 shorter events, 27.6 us)
Async XLA Ops:
  6.5 8.9 %copy-start.17 = (s32[32,5]{0,1:T(8,128)S(1)}, s32[32,5]{0,1:T(8,128)}, u32[]{:S(2)}) copy-start(s32[32,5]{0,1:T(8,128)} %param.5) | copy-start | bytes 1924
  6.5 211.7 %all-gather.3.cloned.1.call-start = ((), (), s32[]{:S(2)}) async-start(), calls=%async_computation | async-start | bytes 10485760 | tf_op jit(solution)/shard_map/all_gather | solution.py:307
  7.8 26.9 %copy-start = (bf16[1024,256]{1,0:T(8,128)(2,1)}, bf16[1024,256]{1,0:T(8,128)(2,1)S(1)}, u32[]{:S(2)}) copy-start(bf16[1024,256]{1,0:T(8,128)(2,1)S(1)} %get-tuple-element.29.refs_1_.refs_0_) | copy-start | bytes 1572868
  7.8 26.9 %copy-start.1 = (bf16[1024,256]{1,0:T(8,128)(2,1)}, bf16[1024,256]{1,0:T(8,128)(2,1)S(1)}, u32[]{:S(2)}) copy-start(bf16[1024,256]{1,0:T(8,128)(2,1)S(1)} %get-tuple-element.30.refs_3_.refs_2_) | copy-start | bytes 1572868
  7.8 14.7 %collective-permute-start.1 = (bf16[1024,256]{1,0:T(8,128)(2,1)S(1)}, bf16[1024,256]{1,0:T(8,128)(2,1)S(1)}, u32[]{:S(2)}, u32[]{:S(2)}) collective-permute-start(bf16[1024,256]{1,0:T(8,128)(2,1)S(1)} %get-tuple-element.29.refs_1_.refs_0_), channel_id=1, source_target_pairs={{4,0},{8,4},{12,8},{16,12},{20,16},{24,20},{28,24},{5,1},{9,5},{13... | collective-permute-start | bytes 1572872 | tf_op jit(solution)/shard_map/ppermute | solution.py:287
  9.1 25.6 %collective-permute-start = (bf16[1024,256]{1,0:T(8,128)(2,1)S(1)}, bf16[1024,256]{1,0:T(8,128)(2,1)S(1)}, u32[]{:S(2)}, u32[]{:S(2)}) collective-permute-start(bf16[1024,256]{1,0:T(8,128)(2,1)S(1)} %get-tuple-element.30.refs_3_.refs_2_), channel_id=1, source_target_pairs={{0,4},{4,8},{8,12},{12,16},{16,20},{20,24},{24,28},{1,5},{5,9},{9,... | collective-permute-start | bytes 1572872 | tf_op jit(solution)/shard_map/ppermute | solution.py:286
  22.5 12.2 %copy-start.9 = (bf16[1024,256]{1,0:T(8,128)(2,1)}, bf16[1024,256]{1,0:T(8,128)(2,1)S(1)}, u32[]{:S(2)}) copy-start(bf16[1024,256]{1,0:T(8,128)(2,1)S(1)} %collective-permute-done.1.refs_4_) | copy-start | bytes 1572868
  43.8 13.8 %copy-start.4 = (bf16[1024,256]{1,0:T(8,128)(2,1)}, bf16[1024,256]{1,0:T(8,128)(2,1)S(1)}, u32[]{:S(2)}) copy-start(bf16[1024,256]{1,0:T(8,128)(2,1)S(1)} %get-tuple-element.37.refs_1_.refs_0_) | copy-start | bytes 1572868
  43.8 13.8 %copy-start.5 = (bf16[1024,256]{1,0:T(8,128)(2,1)}, bf16[1024,256]{1,0:T(8,128)(2,1)S(1)}, u32[]{:S(2)}) copy-start(bf16[1024,256]{1,0:T(8,128)(2,1)S(1)} %get-tuple-element.38.refs_3_.refs_2_) | copy-start | bytes 1572868
  43.9 16.0 %collective-permute-start.3 = (bf16[1024,256]{1,0:T(8,128)(2,1)S(1)}, bf16[1024,256]{1,0:T(8,128)(2,1)S(1)}, u32[]{:S(2)}, u32[]{:S(2)}) collective-permute-start(bf16[1024,256]{1,0:T(8,128)(2,1)S(1)} %get-tuple-element.37.refs_1_.refs_0_), channel_id=1, source_target_pairs={{4,0},{8,4},{12,8},{16,12},{20,16},{24,20},{28,24},{5,1},{9,5},{13... | collective-permute-start | bytes 1572872 | tf_op jit(solution)/shard_map/ppermute | solution.py:287
  45.2 26.6 %collective-permute-start.2 = (bf16[1024,256]{1,0:T(8,128)(2,1)S(1)}, bf16[1024,256]{1,0:T(8,128)(2,1)S(1)}, u32[]{:S(2)}, u32[]{:S(2)}) collective-permute-start(bf16[1024,256]{1,0:T(8,128)(2,1)S(1)} %get-tuple-element.38.refs_3_.refs_2_), channel_id=1, source_target_pairs={{0,4},{4,8},{8,12},{12,16},{16,20},{20,24},{24,28},{1,5},{5,9},{9,... | collective-permute-start | bytes 1572872 | tf_op jit(solution)/shard_map/ppermute | solution.py:286
  59.8 11.9 %copy-start.11 = (bf16[1024,256]{1,0:T(8,128)(2,1)}, bf16[1024,256]{1,0:T(8,128)(2,1)S(1)}, u32[]{:S(2)}) copy-start(bf16[1024,256]{1,0:T(8,128)(2,1)S(1)} %collective-permute-done.3.refs_4_) | copy-start | bytes 1572868
  81.6 13.5 %copy-start.2 = (bf16[1024,256]{1,0:T(8,128)(2,1)}, bf16[1024,256]{1,0:T(8,128)(2,1)S(1)}, u32[]{:S(2)}) copy-start(bf16[1024,256]{1,0:T(8,128)(2,1)S(1)} %get-tuple-element.35.refs_1_.refs_0_) | copy-start | bytes 1572868
  81.6 13.5 %copy-start.3 = (bf16[1024,256]{1,0:T(8,128)(2,1)}, bf16[1024,256]{1,0:T(8,128)(2,1)S(1)}, u32[]{:S(2)}) copy-start(bf16[1024,256]{1,0:T(8,128)(2,1)S(1)} %get-tuple-element.36.refs_3_.refs_2_) | copy-start | bytes 1572868
  81.6 16.0 %collective-permute-start.5 = (bf16[1024,256]{1,0:T(8,128)(2,1)S(1)}, bf16[1024,256]{1,0:T(8,128)(2,1)S(1)}, u32[]{:S(2)}, u32[]{:S(2)}) collective-permute-start(bf16[1024,256]{1,0:T(8,128)(2,1)S(1)} %get-tuple-element.35.refs_1_.refs_0_), channel_id=1, source_target_pairs={{4,0},{8,4},{12,8},{16,12},{20,16},{24,20},{28,24},{5,1},{9,5},{13... | collective-permute-start | bytes 1572872 | tf_op jit(solution)/shard_map/ppermute | solution.py:287
  82.9 26.6 %collective-permute-start.4 = (bf16[1024,256]{1,0:T(8,128)(2,1)S(1)}, bf16[1024,256]{1,0:T(8,128)(2,1)S(1)}, u32[]{:S(2)}, u32[]{:S(2)}) collective-permute-start(bf16[1024,256]{1,0:T(8,128)(2,1)S(1)} %get-tuple-element.36.refs_3_.refs_2_), channel_id=1, source_target_pairs={{0,4},{4,8},{8,12},{12,16},{16,20},{20,24},{24,28},{1,5},{5,9},{9,... | collective-permute-start | bytes 1572872 | tf_op jit(solution)/shard_map/ppermute | solution.py:286
  97.5 11.9 %copy-start.12 = (bf16[1024,256]{1,0:T(8,128)(2,1)}, bf16[1024,256]{1,0:T(8,128)(2,1)S(1)}, u32[]{:S(2)}) copy-start(bf16[1024,256]{1,0:T(8,128)(2,1)S(1)} %collective-permute-done.5.refs_4_) | copy-start | bytes 1572868
  119.5 13.6 %copy-start.6 = (bf16[1024,256]{1,0:T(8,128)(2,1)}, bf16[1024,256]{1,0:T(8,128)(2,1)S(1)}, u32[]{:S(2)}) copy-start(bf16[1024,256]{1,0:T(8,128)(2,1)S(1)} %get-tuple-element.33.refs_1_.refs_0_) | copy-start | bytes 1572868
  119.5 13.6 %copy-start.7 = (bf16[1024,256]{1,0:T(8,128)(2,1)}, bf16[1024,256]{1,0:T(8,128)(2,1)S(1)}, u32[]{:S(2)}) copy-start(bf16[1024,256]{1,0:T(8,128)(2,1)S(1)} %get-tuple-element.34.refs_3_.refs_2_) | copy-start | bytes 1572868
  119.5 20.6 %collective-permute-start.7 = (bf16[1024,256]{1,0:T(8,128)(2,1)S(1)}, bf16[1024,256]{1,0:T(8,128)(2,1)S(1)}, u32[]{:S(2)}, u32[]{:S(2)}) collective-permute-start(bf16[1024,256]{1,0:T(8,128)(2,1)S(1)} %get-tuple-element.33.refs_1_.refs_0_), channel_id=1, source_target_pairs={{4,0},{8,4},{12,8},{16,12},{20,16},{24,20},{28,24},{5,1},{9,5},{13... | collective-permute-start | bytes 1572872 | tf_op jit(solution)/shard_map/ppermute | solution.py:287
  120.8 26.6 %collective-permute-start.6 = (bf16[1024,256]{1,0:T(8,128)(2,1)S(1)}, bf16[1024,256]{1,0:T(8,128)(2,1)S(1)}, u32[]{:S(2)}, u32[]{:S(2)}) collective-permute-start(bf16[1024,256]{1,0:T(8,128)(2,1)S(1)} %get-tuple-element.34.refs_3_.refs_2_), channel_id=1, source_target_pairs={{0,4},{4,8},{8,12},{12,16},{16,20},{20,24},{24,28},{1,5},{5,9},{9,... | collective-permute-start | bytes 1572872 | tf_op jit(solution)/shard_map/ppermute | solution.py:286
  148.2 8.8 %copy-start.8 = (bf16[2048,256]{1,0:T(8,128)(2,1)S(1)}, bf16[2048,256]{1,0:T(8,128)(2,1)}, u32[]{:S(2)}) copy-start(bf16[2048,256]{1,0:T(8,128)(2,1)} %shard_map.44) | copy-start | bytes 3145732
  158.4 141.0 %all-reduce.2.cloned.1.call-start = ((), (), s32[]{:S(2)}) async-start(), calls=%async_computation.1 | async-start | bytes 1310720 | tf_op jit(solution)/shard_map/psum | solution.py:311
  226.6 100.0 %all-gather.5.cloned.1.call-start = ((), (), s32[]{:S(2)}) async-start(), calls=%async_computation.2 | async-start | bytes 3276800 | tf_op jit(solution)/shard_map/all_gather | solution.py:312
  (5 other events, 10.5 us)
Sparse Core Ops, SparseCore 0:
  158.6 59.6 all-gather.2
  226.7 72.7 all-reduce.1
  301.1 25.3 all-gather.4
where the time goes:
time: 416 us; the launch traced here: 413 us
  waiting for transfers between devices  213 us (51%)
  Pallas kernels  125 us (30%)
  starting transfers between devices  23.6 us (6%)
  matrix products  21.2 us (5%)
  local copies, waits for them, and re-layouts  13.8 us (3%)
  between operations  13.4 us (3%)
    psum x1, waiting for transfers between devices, shards(): summed = lax.psum(panel_part(panel), 'rows')  72.9 us
    pallas_call x1, Pallas kernels, inverse_factor(): pl.pallas_call(functools.partial(inverse_kernel, size, total_rows, panels...  65.6 us
    all_gather x1, waiting for transfers between devices, shards(): whole_block = lax.all_gather(final, 'vecs', axis=1, tiled=True)  59.8 us
    pallas_call x8, Pallas kernels, chebyshev_step(): pl.pallas_call(functools.partial(step_kernel, group, len(pieces), kind, e...  58.9 us
    ppermute x4, waiting for transfers between devices, filtered_block(): before = lax.ppermute(high, 'rows', up)  43.3 us
    all_gather x1, waiting for transfers between devices, shards(): gram = lax.all_gather(summed, 'vecs', axis=0, tiled=True)  27.1 us
    ppermute x4, starting transfers between devices, filtered_block(): before = lax.ppermute(high, 'rows', up)  18.3 us
    ppermute x4, waiting for transfers between devices, filtered_block(): after = lax.ppermute(low, 'rows', down)  9.78 us
  transfers between devices with their start and end apart: 11, of which 10 were waited for; matrix products, arithmetic and copies ran while one was open for 1% of the time, Pallas kernels for 7%

commit v1 on v0

--- a/solution.py
+++ b/solution.py
@@ -17,83 +17,171 @@
 PIVOTS = 8
 
 
-def step_kernel(group, n_pieces, kind, emit_f32, index_ref, *refs):
-    pieces = refs[:n_pieces]
-    blocks_ref = refs[n_pieces]
-    rest = refs[n_pieces + 1 :]
-    if kind == "first":
-        (cur_ref, *outs), old_ref = rest, None
-    else:
-        cur_ref, old_ref, *outs = rest
-    *outs, window = outs
-    step = pl.program_id(0)
-    size_b = blocks_ref.shape[2]
-    nnz = blocks_ref.shape[1]
-
-    @pl.when(step == 0)
-    def _():
-        start = 0
-        for piece in pieces:
-            count = piece.shape[0]
-            window[start : start + count, :] = piece[...]
-            start += count
-
-    for g in range(group):
-        acc = None
-        for j in range(nnz):
-            at = pl.multiple_of(index_ref[(step * group + g) * nnz + j] * size_b, size_b)
-            part = jnp.dot(
-                blocks_ref[g, j], window[pl.ds(at, size_b), :], preferred_element_type=jnp.float32
-            )
-            acc = part if acc is None else acc + part
-        rows = slice(g * size_b, (g + 1) * size_b)
-        cur = cur_ref[rows, :].astype(jnp.float32)
-        new = (acc - filter_center * cur) * (1.0 / filter_radius)
-        if kind != "first":
-            new = 2.0 * new - old_ref[rows, :].astype(jnp.float32)
-        outs[0][rows, :] = new.astype(jnp.bfloat16)
-        if emit_f32:
-            outs[1][rows, :] = new
-
-
-def chebyshev_step(index, pieces, blocks, row_of, count, cur, old, kind, emit_f32):
-    size_b, nnz = blocks.shape[2], blocks.shape[1]
-    width = pieces[0].shape[1]
-    group = 4 if count % 4 == 0 else 1
-    whole = lambda i, ix: (0, 0)
-    part = lambda i, ix: (i, 0)
-    tall = (group * size_b, width)
-    in_specs = [pl.BlockSpec(p.shape, whole) for p in pieces]
-    in_specs.append(
-        pl.BlockSpec((group, nnz, size_b, size_b), lambda i, ix: (row_of(i, group), 0, 0, 0))
-    )
-    operands = list(pieces) + [blocks, cur]
-    in_specs.append(pl.BlockSpec(tall, part))
-    if kind != "first":
-        operands.append(old)
-        in_specs.append(pl.BlockSpec(tall, part))
-    rows = count * size_b
-    out_shape = [jax.ShapeDtypeStruct((rows, width), jnp.bfloat16)]
-    if emit_f32:
-        out_shape.append(jax.ShapeDtypeStruct((rows, width), jnp.float32))
-    window_rows = sum(p.shape[0] for p in pieces)
-    return pl.pallas_call(
-        functools.partial(step_kernel, group, len(pieces), kind, emit_f32),
-        grid_spec=pltpu.PrefetchScalarGridSpec(
-            num_scalar_prefetch=1,
-            grid=(count // group,),
-            in_specs=in_specs,
-            out_specs=[pl.BlockSpec(tall, part) for _ in out_shape],
-            scratch_shapes=[pltpu.VMEM((window_rows, width), jnp.bfloat16)],
+def filter_kernel(
+    place_ref, vectors_ref, blocks_ref, out_ref,
+    first_win, even_win, odd_win, top_a, top_b, bottom_a, bottom_b, even, odd, held,
+    in_sem, send_sem, recv_sem,
+):
+    me, count = lax.axis_index("rows"), lax.axis_size("rows")
+    block_rows, nnz = blocks_ref.shape[:2]
+    reach = block_rows // 4
+    span = 2 * reach
+    top, bottom = (top_a, top_b), (bottom_a, bottom_b)
+
+    @pl.when(me > 0)
+    def _():
+        pl.semaphore_signal(pltpu.get_barrier_semaphore(), 1, device_id={"rows": me - 1})
+
+    @pl.when(me < count - 1)
+    def _():
+        pl.semaphore_signal(pltpu.get_barrier_semaphore(), 1, device_id={"rows": me + 1})
+
+    fetches = [
+        pltpu.make_async_copy(vectors_ref, first_win, in_sem.at[0]),
+        pltpu.make_async_copy(vectors_ref.at[:span], top_a.at[reach:], in_sem.at[1]),
+        pltpu.make_async_copy(vectors_ref.at[block_rows - span :], bottom_a.at[:span], in_sem.at[2]),
+        pltpu.make_async_copy(blocks_ref, held, in_sem.at[3]),
+    ]
+    for fetch in fetches:
+        fetch.start()
+
+    inside = jnp.logical_and(me > 0, me < count - 1)
+
+    @pl.when(inside)
+    def _():
+        pl.semaphore_wait(pltpu.get_barrier_semaphore(), 2)
+
+    @pl.when(jnp.logical_not(inside))
+    def _():
+        pl.semaphore_wait(pltpu.get_barrier_semaphore(), 1)
+
+    def to_lower(source, slot):
+        return pltpu.make_async_remote_copy(
+            src_ref=source.at[:reach], dst_ref=bottom[slot].at[span:],
+            send_sem=send_sem.at[0, slot], recv_sem=recv_sem.at[0, slot],
+            device_id={"rows": me - 1},
+        )
+
+    def to_upper(source, slot):
+        return pltpu.make_async_remote_copy(
+            src_ref=source.at[block_rows - reach :], dst_ref=top[slot].at[:reach],
+            send_sem=send_sem.at[1, slot], recv_sem=recv_sem.at[1, slot],
+            device_id={"rows": me + 1},
+        )
+
+    @pl.when(me > 0)
+    def _():
+        to_lower(vectors_ref, 0).start()
+
+    @pl.when(me < count - 1)
+    def _():
+        to_upper(vectors_ref, 0).start()
+
+    for fetch in fetches:
+        fetch.wait()
+
+    windows = [first_win, odd_win, even_win, odd_win, even_win]
+    states = [None, even, odd, even, None]
+
+    def compute(step, start, stop, window, group=4):
+        slot = (step + 1) % 2
+        target = windows[step + 1]
+        last = step == DEGREE - 1
+
+        @pl.loop(0, (stop - start) // group)
+        def _(index):
+            for g in range(group):
+                row = start + index * group + g
+                acc = None
+                for j in range(nnz):
+                    part = jnp.dot(
+                        held[row, j], window[place_ref[row, j]], preferred_element_type=jnp.float32
+                    )
+                    acc = part if acc is None else acc + part
+                cur = first_win[row].astype(jnp.float32) if step == 0 else states[step][row]
+                new = (acc - filter_center * cur) * (1.0 / filter_radius)
+                if step == 1:
+                    new = 2.0 * new - first_win[row].astype(jnp.float32)
+                elif step > 1:
+                    new = 2.0 * new - states[step - 1][row]
+                rounded = new.astype(jnp.bfloat16)
+                target[row] = rounded
+                if not last:
+                    states[step + 1][row] = new
+                    if stop <= span:
+                        top[slot][row + reach] = rounded
+                    if start >= span:
+                        bottom[slot][row - span] = rounded
+
+    for step in range(DEGREE):
+        now = step % 2
+        later = 1 - now
+        source = vectors_ref if step == 0 else windows[step]
+        compute(step, reach, 2 * reach, windows[step])
+        compute(step, 2 * reach, 3 * reach, windows[step])
+
+        @pl.when(me < count - 1)
+        def _():
+            to_lower(source, now).wait_recv()
+
+        compute(step, 3 * reach, 4 * reach, bottom[now])
+        if step < DEGREE - 1:
+
+            @pl.when(me < count - 1)
+            def _():
+                to_upper(windows[step + 1], later).start()
+
+        @pl.when(me > 0)
+        def _():
+            to_upper(source, now).wait_recv()
+
+        compute(step, 0, reach, top[now])
+        if step < DEGREE - 1:
+
+            @pl.when(me > 0)
+            def _():
+                to_lower(windows[step + 1], later).start()
+
+        @pl.when(me > 0)
+        def _():
+            to_lower(source, now).wait_send()
+
+        @pl.when(me < count - 1)
+        def _():
+            to_upper(source, now).wait_send()
+
+    done = pltpu.make_async_copy(windows[DEGREE], out_ref, in_sem.at[0])
+    done.start()
+    done.wait()
+
+
+def filtered_block(vectors, blocks, columns):
+    rows, width = vectors.shape
+    block_rows, nnz, size_b = blocks.shape[:3]
+    reach = block_rows // 4
+    row = lax.broadcasted_iota(jnp.int32, columns.shape, 0)
+    shift = jnp.where(row < reach, reach, jnp.where(row < block_rows - reach, 0, -2 * reach))
+    place = columns - lax.axis_index("rows") * block_rows + shift
+    window = pltpu.VMEM((block_rows, size_b, width), jnp.bfloat16)
+    side = pltpu.VMEM((3 * reach, size_b, width), jnp.bfloat16)
+    state = pltpu.VMEM((block_rows, size_b, width), jnp.float32)
+    anywhere = pl.BlockSpec(memory_space=pl.ANY)
+    out = pl.pallas_call(
+        filter_kernel,
+        out_shape=jax.ShapeDtypeStruct((block_rows, size_b, width), jnp.bfloat16),
+        in_specs=[pl.BlockSpec(memory_space=pltpu.SMEM), anywhere, anywhere],
+        out_specs=anywhere,
+        scratch_shapes=[window] * 3 + [side] * 4 + [state] * 2 + [
+            pltpu.VMEM(blocks.shape, jnp.bfloat16),
+            pltpu.SemaphoreType.DMA((4,)),
+            pltpu.SemaphoreType.DMA((2, 2)),
+            pltpu.SemaphoreType.DMA((2, 2)),
+        ],
+        compiler_params=pltpu.CompilerParams(
+            vmem_limit_bytes=VMEM_LIMIT, collective_id=0, has_side_effects=True
         ),
-        out_shape=out_shape,
-        compiler_params=pltpu.CompilerParams(vmem_limit_bytes=VMEM_LIMIT),
-        cost_estimate=pl.CostEstimate(
-            flops=2 * rows * nnz * size_b * width,
-            bytes_accessed=rows * nnz * size_b * 2 + rows * width * 16,
-            transcendentals=0,
-        ),
-    )(index, *operands)
+    )(place, vectors.reshape(block_rows, size_b, width), blocks)
+    return out.reshape(rows, width)
 
 
 def factor_block(block):
@@ -252,54 +340,6 @@
     return first + second
 
 
-def filtered_block(vectors, blocks, columns):
-    block_rows, nnz, size_b = blocks.shape[:3]
-    reach = block_rows // 4
-    edge = reach * size_b
-    first_row = lax.axis_index("rows") * block_rows
-    local = columns - first_row
-    edges_index = jnp.concatenate([local[:reach], local[block_rows - reach :]], axis=0) + reach
-    edges_index = edges_index.reshape(-1)
-    inner_index = local[reach : block_rows - reach].reshape(-1)
-    inner_rows = block_rows - 2 * reach
-
-    axis_size = lax.axis_size("rows")
-    up = [(i, i + 1) for i in range(axis_size - 1)]
-    down = [(j, i) for i, j in up]
-
-    def inner_of(i, group):
-        return i + reach // group
-
-    def edges_of(i, group):
-        return jnp.where(i < reach // group, i, i + inner_rows // group)
-
-    def halves(array):
-        return jnp.concatenate([array[:edge], array[-edge:]], axis=0), array[edge:-edge]
-
-    cur_edges, cur_inner = halves(vectors)
-    bf_edges, bf_inner = cur_edges, cur_inner
-    old_edges = old_inner = None
-    for iteration in range(DEGREE):
-        kind = "first" if iteration == 0 else "next"
-        emit_f32 = iteration < DEGREE - 1
-        low, high = bf_edges[:edge], bf_edges[edge:]
-        before = lax.ppermute(high, "rows", up)
-        after = lax.ppermute(low, "rows", down)
-        own = [low, bf_inner, high]
-        new_inner = chebyshev_step(
-            inner_index, own, blocks, inner_of, inner_rows, cur_inner, old_inner, kind, emit_f32
-        )
-        new_edges = chebyshev_step(
-            edges_index, [before] + own + [after], blocks, edges_of, 2 * reach,
-            cur_edges, old_edges, kind, emit_f32,
-        )
-        old_edges, old_inner = cur_edges, cur_inner
-        bf_edges, bf_inner = new_edges[0], new_inner[0]
-        if emit_f32:
-            cur_edges, cur_inner = new_edges[1], new_inner[1]
-    return jnp.concatenate([bf_edges[:edge], bf_inner, bf_edges[edge:]], axis=0)
-
-
 def shards(vectors, blocks, columns):
     total_rows = vectors.shape[0] * lax.axis_size("rows")
     final = filtered_block(vectors, blocks, columns)

time: 416 us -> 382 us (0.918)
  starting transfers between devices: 23.6 us -> 0.09 us
  Pallas kernels: 125 us -> 148 us
  waiting for transfers between devices: 213 us -> 194 us
  local copies, waits for them, and re-layouts: 13.8 us -> 1.06 us
    ppermute x8 -> x0, waiting for transfers between devices: 53.1 us -> none  [the longest x4 43.3 us: filtered_block(): before = lax.ppermute(high, 'rows', up)]
    all_gather x1, waiting for transfers between devices: 59.8 us -> 94 us  [shards(): whole_block = lax.all_gather(final, 'vecs', axis=1, tiled=True)]
    ppermute x8 -> x0, starting transfers between devices: 23.5 us -> none  [the longest x4 18.3 us: filtered_block(): before = lax.ppermute(high, 'rows', up)]
    pallas_call x8 -> x1, Pallas kernels: 58.9 us -> 82.1 us  [filtered_block(): pl.pallas_call(filter_kernel, out_shape=jax.ShapeDtypeStruct((block_rows,...]
    slice x9 -> x0, local copies, waits for them, and re-layouts: 8.86 us -> none  [the longest x3 3.8 us: filtered_block(): low, high = (bf_edges[:edge], bf_edges[edge:])]
  transfers between devices with their start and end apart: 11 -> 3, of which waited for: 10 -> 3; matrix products, arithmetic and copies ran while one was open for 1% -> 0% of each run, Pallas kernels for 7% -> 0%
where the time goes in v1:
time: 382 us; the launch traced here: 380 us
  waiting for transfers between devices  194 us (51%)
  Pallas kernels  148 us (39%)
  matrix products  21.8 us (6%)
  between operations  13.2 us (3%)
    all_gather x1, waiting for transfers between devices, shards(): whole_block = lax.all_gather(final, 'vecs', axis=1, tiled=True)  94 us
    pallas_call x1, Pallas kernels, filtered_block(): pl.pallas_call(filter_kernel, out_shape=jax.ShapeDtypeStruct((block_rows,...  82.1 us
    psum x1, waiting for transfers between devices, shards(): summed = lax.psum(panel_part(panel), 'rows')  72.9 us
    pallas_call x1, Pallas kernels, inverse_factor(): pl.pallas_call(functools.partial(inverse_kernel, size, total_rows, panels...  65.6 us
    all_gather x1, waiting for transfers between devices, shards(): gram = lax.all_gather(summed, 'vecs', axis=0, tiled=True)  27.1 us
    dot_general x1, matrix products, split_apply(): second = jnp.dot(left_bf, factor_low.T, preferred_element_type=jnp.float32)  8.34 us
  transfers between devices with their start and end apart: 3, of which 3 were waited for; matrix products, arithmetic and copies ran while one was open for 0% of the time, Pallas kernels for 0%

profile of v1, /device:TPU:3, one launch (start us, length us, event | category | flops | bytes accessed | tf_op | source)
XLA Modules:
  0.0 379.7 jit_solution(13594556857672915322)
XLA Ops:
  6.5 0.0 all-gather.3.cloned.1.call-start
  6.6 0.8 copy.9
  7.3 0.7 select_add_fusion.place_ref
  8.0 82.1 %shard_map.37 = bf16[32,128,256]{2,1,0:T(8,128)(2,1)} custom-call(s32[32,5]{1,0:T(8,128)} %select_add_fusion.place_ref, bf16[32,128,256]{2,1,0:T(8,128)(2,1)} %bitcast.12, bf16[32,5,128,128]{3,2,1,0:T(8,128)(2,1)} %blocks_ref.1), custom_call_target="tpu_custom_call" | custom-call | tf_op jit(solution)/shard_map/pallas_call | solution.py:169
  90.1 0.0 all-gather.3.cloned.1.call-update
  90.1 0.0 all-reduce.2.cloned.1.call-start
  90.2 94.0 %all-gather.3.cloned.1.call-done = bf16[4096,1024]{1,0:T(8,128)(2,1)} async-done(((bf16[4096,256]{1,0:T(8,128)(2,1)}), bf16[4096,1024]{1,0:T(8,128)(2,1)}) %all-gather.3.cloned.1.call-update) | async-done | bytes 8388624 | tf_op jit(solution)/shard_map/all_gather | solution.py:347
  184.2 7.4 %fusion.6 = f32[256,1024]{0,1:T(8,128)S(1)} fusion(bf16[4096,256]{1,0:T(8,128)(2,1)} %bitcast.11, bf16[4096,1024]{1,0:T(8,128)(2,1)} %all-gather.3.cloned.1.call-done), kind=kOutput, calls=%fused_computation.18 | convolution fusion | flops 2147483648 | bytes 11534336 | tf_op jit(solution)/shard_map/dot_general | solution.py:348
  191.5 0.1 fusion.1
  191.6 0.2 fusion
  191.8 0.2 copy.14
  192.1 0.1 copy.13
  192.2 0.9 pad_maximum_fusion
  193.1 0.0 all-reduce.2.cloned.1.call-update
  193.1 0.0 all-gather.5.cloned.1.call-start
  193.1 72.9 %all-reduce.2.cloned.1.call-done = f32[256,640]{1,0:T(8,128)} async-done(((f32[256,640]{1,0:T(8,128)}), f32[256,640]{1,0:T(8,128)}) %all-reduce.2.cloned.1.call-update) | async-done | bytes 655376 | tf_op jit(solution)/shard_map/psum | solution.py:351
  266.0 0.0 all-gather.5.cloned.1.call-update
  266.1 27.1 %all-gather.5.cloned.1.call-done.gram_ref = f32[1024,640]{1,0:T(8,128)} async-done(((f32[256,640]{1,0:T(8,128)}), f32[1024,640]{1,0:T(8,128)}) %all-gather.5.cloned.1.call-update) | async-done | bytes 2621456 | tf_op jit(solution)/shard_map/all_gather | solution.py:352
  293.1 65.6 %shard_map.38 = f32[1024,1024]{1,0:T(8,128)} custom-call(f32[1024,640]{1,0:T(8,128)} %all-gather.5.cloned.1.call-done.gram_ref), custom_call_target="tpu_custom_call" | custom-call | flops 42949672960 | bytes 8388608 | tf_op jit(solution)/shard_map/pallas_call | solution.py:319
  358.7 6.1 %fusion.2 = f32[4096,256]{1,0:T(8,128)S(1)} fusion(bf16[4096,1024]{1,0:T(8,128)(2,1)} %all-gather.3.cloned.1.call-done, f32[1024,1024]{1,0:T(8,128)} %shard_map.38, s32[]{:T(128)S(6)} %select_n.32), kind=kOutput, calls=%fused_computation.10 | convolution fusion | flops 2147483648 | bytes 13107204 | tf_op jit(solution)/shard_map/dot_general | solution.py:338
  364.8 8.3 %convolution_add_fusion = f32[4096,256]{1,0:T(8,128)} fusion(f32[4096,256]{1,0:T(8,128)S(1)} %fusion.2, bf16[4096,1024]{1,0:T(8,128)(2,1)} %all-gather.3.cloned.1.call-done, f32[1024,1024]{1,0:T(8,128)} %shard_map.38, s32[]{:T(128)S(6)} %select_n.32), kind=kOutput, calls=%fused_computation | convolution fusion | flops 2149580800 | bytes 17825796 | tf_op jit(solution)/shard_map/dot_general | solution.py:339
  (4 shorter events, 0.0 us)
Async XLA Ops:
  6.5 177.6 %all-gather.3.cloned.1.call-start = ((), (), s32[]{:S(2)}) async-start(), calls=%async_computation | async-start | bytes 10485760 | tf_op jit(solution)/shard_map/all_gather | solution.py:347
  90.1 175.9 %all-reduce.2.cloned.1.call-start = ((), (), s32[]{:S(2)}) async-start(), calls=%async_computation.1 | async-start | bytes 1310720 | tf_op jit(solution)/shard_map/psum | solution.py:351
  193.1 100.0 %all-gather.5.cloned.1.call-start = ((), (), s32[]{:S(2)}) async-start(), calls=%async_computation.2 | async-start | bytes 3276800 | tf_op jit(solution)/shard_map/all_gather | solution.py:352
Sparse Core Ops, SparseCore 0:
  90.2 93.8 all-gather.2
  193.2 72.7 all-reduce.1
  267.7 25.3 all-gather.4

commit v2 on v1

--- a/solution.py
+++ b/solution.py
@@ -231,29 +231,267 @@
     return jnp.concatenate(tiles, axis=0)
 
 
-def inverse_kernel(size, total_rows, panels, gram_ref, out_ref, work, factor):
-    full = gram_ref.shape[0]
-    count = full // size
-    wide = full // panels
-    half = panels // 2
+def gram_stages(rows, devices):
+    stages, bit, held = [], 1, rows
+    while bit < devices:
+        halve = held % 16 == 0
+        stages.append((bit, halve))
+        held, bit = held // 2 if halve else held, bit * 2
+    return stages
+
+
+def flipped(index, bit):
+    return index + bit - 2 * bit * lax.rem(index // bit, 2)
+
+
+def gram_kernel(
+    stages, final_ref, out_ref, own, beside, across, far, cross, total, full, landing, cross_in,
+    local_sem, side_send, side_recv, x_send, x_recv, pass_send, pass_recv, stage_sem, all_send, all_recv,
+):
+    me, panel = lax.axis_index("rows"), lax.axis_index("vecs")
+    core, side = lax.rem(panel, 2), panel // 2
+    rows, wide = own.shape
+    half, short = rows // 2, wide // 2
+    parts = across.shape[0]
+    chunk = half // parts
+    near, over = flipped(panel, 1), flipped(panel, 2)
+    contract = (((0,), (0,)), ((), ()))
+
+    peers = [{"vecs": near}, {"vecs": over}] + [{"rows": flipped(me, bit)} for bit, _ in stages]
+    barrier = pltpu.get_barrier_semaphore()
+    for peer in peers:
+        pl.semaphore_signal(barrier, 1, device_id=peer)
+    fetch = pltpu.make_async_copy(final_ref, own, local_sem.at[0])
+    fetch.start()
+    pl.semaphore_wait(barrier, len(peers))
+    fetch.wait()
+
+    to_over, to_near, passed = [], [], []
+    for part in range(parts):
+        start = pl.multiple_of((1 - side) * half + part * chunk, chunk)
+        to_over.append(
+            pltpu.make_async_remote_copy(
+                src_ref=own.at[pl.ds(start, chunk)], dst_ref=across.at[part],
+                send_sem=x_send.at[part], recv_sem=x_recv.at[part], device_id={"vecs": over},
+            )
+        )
+        passed.append(
+            pltpu.make_async_remote_copy(
+                src_ref=across.at[part], dst_ref=far.at[part],
+                send_sem=pass_send.at[part], recv_sem=pass_recv.at[part], device_id={"vecs": near},
+            )
+        )
+    for copy in to_over:
+        copy.start()
+    for part in range(2):
+        to_near.append(
+            pltpu.make_async_remote_copy(
+                src_ref=own.at[part * half : (part + 1) * half], dst_ref=beside.at[part],
+                send_sem=side_send.at[part], recv_sem=side_recv.at[part], device_id={"vecs": near},
+            )
+        )
+        to_near[-1].start()
+
+    def product(left, right):
+        return lax.dot_general(left, right, contract, preferred_element_type=jnp.float32)
+
+    total[: wide + short, :] = jnp.zeros((wide + short, wide), jnp.float32)
+    cross[...] = jnp.zeros_like(cross)
+
+    @pl.loop(0, rows // chunk)
+    def _(index):
+        at = pl.ds(pl.multiple_of(index * chunk, chunk), chunk)
+        total[:wide, :] += product(own[at, :], own[at, :])
+
+    for copy in to_near:
+        copy.wait()
+    for part in range(2):
+
+        @pl.loop(0, parts)
+        def _(index):
+            at = pl.ds(pl.multiple_of(index * chunk, chunk), chunk)
+            mine = pl.ds(pl.multiple_of(part * half + index * chunk, chunk), chunk)
+
+            @pl.when(core == 0)
+            def _():
+                total[wide : wide + short, :] += product(own[mine, :short], beside[part, at, :])
+
+            @pl.when(core == 1)
+            def _():
+                total[wide : wide + short, :] += product(beside[part, at, short:], own[mine, :])
+
+    for part in range(parts):
+        to_over[part].wait()
+        at = slice(part * chunk, (part + 1) * chunk)
+
+        @pl.when(side == 0)
+        def _():
+            passed[part].start()
+            mine = own[at, :]
+
+            @pl.when(core == 0)
+            def _():
+                cross[0] += product(mine, across[part])
+
+            @pl.when(core == 1)
+            def _():
+                cross[1] += product(mine, across[part])
+
+        @pl.when(side == 1)
+        def _():
+            there = across[part]
+            later = slice(half + part * chunk, half + (part + 1) * chunk)
+
+            @pl.when(core == 0)
+            def _():
+                cross[0] += product(there, own[later, :])
+                cross[1] += product(there, beside[1, at, :])
+
+            @pl.when(core == 1)
+            def _():
+                cross[0] += product(there, beside[1, at, :])
+                cross[1] += product(there, own[later, :])
+
+    @pl.when(side == 0)
+    def _():
+        for part in range(parts):
+            passed[part].wait()
+            mine = own[part * chunk : (part + 1) * chunk, :]
+
+            @pl.when(core == 0)
+            def _():
+                cross[1] += product(mine, far[part])
+
+            @pl.when(core == 1)
+            def _():
+                cross[0] += product(mine, far[part])
+
+    swap = pltpu.make_async_remote_copy(
+        src_ref=cross.at[1 - side], dst_ref=cross_in,
+        send_sem=local_sem.at[1], recv_sem=local_sem.at[2], device_id={"vecs": over},
+    )
+    swap.start()
+    swap.wait()
+    total[wide + short :, :] = cross[side] + cross_in[...]
+
+    start, held, taken = 0, total.shape[0], 0
+    ranges = []
+    for number, (bit, halve) in enumerate(stages):
+        size = held // 2 if halve else held
+        upper = lax.rem(me // bit, 2)
+        ranges.append((start, size))
+        keep = pl.multiple_of(start + upper * size, 8) if halve else start
+        give = pl.multiple_of(start + (1 - upper) * size, 8) if halve else start
+        slot = landing.at[taken : taken + size]
+        copy = pltpu.make_async_remote_copy(
+            src_ref=total.at[pl.ds(give, size)], dst_ref=slot,
+            send_sem=stage_sem.at[0, number], recv_sem=stage_sem.at[1, number],
+            device_id={"rows": flipped(me, bit)},
+        )
+        copy.start()
+        copy.wait()
+        total[pl.ds(keep, size), :] += landing[taken : taken + size, :]
+        start, held, taken = keep, size, taken + size
+
+    full[panel, pl.ds(start, held), :] = total[pl.ds(start, held), :]
+    pending = []
+
+    def share(number, first, size):
+        piece = full.at[panel, pl.ds(first, size)]
+        copies = []
+        for kind, peer in enumerate((over, near)):
+            copies.append(
+                pltpu.make_async_remote_copy(
+                    src_ref=piece, dst_ref=piece, send_sem=all_send.at[kind, number],
+                    recv_sem=all_recv.at[kind, number], device_id={"vecs": peer},
+                )
+            )
+            copies[-1].start()
+        theirs = full.at[over, pl.ds(first, size)]
+        onward = pltpu.make_async_remote_copy(
+            src_ref=theirs, dst_ref=theirs, send_sem=all_send.at[2, number],
+            recv_sem=all_recv.at[2, number], device_id={"vecs": near},
+        )
+        pending.append((copies, onward))
+
+    share(0, start, held)
+    count = 1
+    for number in reversed(range(len(stages))):
+        bit, halve = stages[number]
+        if not halve:
+            continue
+        upper = lax.rem(me // bit, 2)
+        below, size = ranges[number]
+        mine = pl.multiple_of(below + upper * size, 8)
+        other = pl.multiple_of(below + (1 - upper) * size, 8)
+        piece = full.at[panel, pl.ds(mine, size)]
+        copy = pltpu.make_async_remote_copy(
+            src_ref=piece, dst_ref=piece, send_sem=stage_sem.at[2, number],
+            recv_sem=stage_sem.at[3, number], device_id={"rows": flipped(me, bit)},
+        )
+        copy.start()
+        copy.wait()
+        share(count, other, size)
+        count += 1
+    for copies, onward in pending:
+        copies[0].wait()
+        onward.start()
+        copies[1].wait()
+    for _, onward in pending:
+        onward.wait()
+    done = pltpu.make_async_copy(full, out_ref, local_sem.at[3])
+    done.start()
+    done.wait()
+
+
+def gram_sum(final):
+    rows, wide = final.shape
+    panels, devices = lax.axis_size("vecs"), lax.axis_size("rows")
+    tall = 2 * wide + wide // 2
+    stages = gram_stages(tall, devices)
+    parts = 4
+    chunk = rows // 2 // parts
+    dma = pltpu.SemaphoreType.DMA
+    steps = len(stages)
+    return pl.pallas_call(
+        functools.partial(gram_kernel, stages),
+        out_shape=jax.ShapeDtypeStruct((panels, tall, wide), jnp.float32),
+        in_specs=[pl.BlockSpec(memory_space=pl.ANY)],
+        out_specs=pl.BlockSpec(memory_space=pl.ANY),
+        scratch_shapes=[
+            pltpu.VMEM((rows, wide), jnp.bfloat16),
+            pltpu.VMEM((2, rows // 2, wide), jnp.bfloat16),
+            pltpu.VMEM((parts, chunk, wide), jnp.bfloat16),
+            pltpu.VMEM((parts, chunk, wide), jnp.bfloat16),
+            pltpu.VMEM((2, wide, wide), jnp.float32),
+            pltpu.VMEM((tall, wide), jnp.float32),
+            pltpu.VMEM((panels, tall, wide), jnp.float32),
+            pltpu.VMEM((2 * tall, wide), jnp.float32),
+            pltpu.VMEM((wide, wide), jnp.float32),
+            dma((4,)), dma((2,)), dma((2,)), dma((parts,)), dma((parts,)), dma((parts,)), dma((parts,)),
+            dma((4, steps)), dma((3, steps + 1)), dma((3, steps + 1)),
+        ],
+        compiler_params=pltpu.CompilerParams(
+            vmem_limit_bytes=VMEM_LIMIT, collective_id=1, has_side_effects=True
+        ),
+    )(final)
+
+
+def inverse_kernel(size, total_rows, gram_ref, out_ref, work, factor):
+    full = out_ref.shape[0]
+    panels, _, wide = gram_ref.shape
+    count, short = full // size, wide // 2
     work[...] = jnp.zeros_like(work)
-    for low in range(panels):
-        for high in range(low, panels):
-            apart = high - low
-            own, other = slice(low * wide, (low + 1) * wide), slice(high * wide, (high + 1) * wide)
-            if not shared(panels, wide):
-                work[own, other] = gram_ref[own, other] / total_rows
-            elif apart < half:
-                work[own, other] = gram_ref[own, apart * wide : (apart + 1) * wide] / total_rows
-            elif apart > half:
-                back = panels - apart
-                part = gram_ref[other, back * wide : (back + 1) * wide] / total_rows
-                work[own, other] = part.T
-            else:
-                middle = high * wide + wide // 2
-                last = slice(half * wide, half * wide + wide // 2)
-                work[own, high * wide : middle] = gram_ref[own, last] / total_rows
-                work[own, middle : (high + 1) * wide] = gram_ref[other, last] / total_rows
+    for panel in range(panels):
+        core, side = panel % 2, panel // 2
+        own = slice(panel * wide, (panel + 1) * wide)
+        work[own, own] = gram_ref[panel, :wide, :] / total_rows
+        first = 2 * side * wide
+        high = slice(first + core * short, first + (core + 1) * short)
+        work[high, first + wide : first + 2 * wide] = gram_ref[panel, wide : wide + short, :] / total_rows
+        low = slice(core * wide, (core + 1) * wide)
+        other = slice((2 + side) * wide, (3 + side) * wide)
+        work[low, other] = gram_ref[panel, wide + short :, :] / total_rows
 
     @pl.loop(0, count)
     def _(k):
@@ -297,27 +535,11 @@
                     work[below, own] = -change[:, c * size :]
 
 
-def shared(panels, wide):
-    return panels % 2 == 0 and wide % 256 == 0
-
-
-def panel_part(panel):
-    panels, wide = lax.axis_size("vecs"), panel.shape[0]
-    if not shared(panels, wide):
-        return panel
-    me, half, short = lax.axis_index("vecs"), panels // 2, wide // 2
-    twice = jnp.concatenate([panel, panel], axis=1)
-    near = lax.dynamic_slice_in_dim(twice, me * wide, half * wide, 1)
-    far = lax.dynamic_slice_in_dim(twice, (me + half) * wide, wide, 1)
-    middle = jnp.where(me < half, far[:, :short], far[short:, :].T)
-    return jnp.concatenate([near, middle], axis=1)
-
-
-def inverse_factor(gram, total_rows, panels):
-    full = gram.shape[0]
+def inverse_factor(gram, total_rows):
+    full = gram.shape[0] * gram.shape[2]
     size = 128
     return pl.pallas_call(
-        functools.partial(inverse_kernel, size, total_rows, panels),
+        functools.partial(inverse_kernel, size, total_rows),
         out_shape=jax.ShapeDtypeStruct((full, full), jnp.float32),
         in_specs=[pl.BlockSpec(memory_space=pltpu.VMEM)],
         out_specs=pl.BlockSpec(memory_space=pltpu.VMEM),
@@ -344,13 +566,10 @@
     total_rows = vectors.shape[0] * lax.axis_size("rows")
     final = filtered_block(vectors, blocks, columns)
     panel_width = final.shape[1]
+    gram = gram_sum(final)
+    final, gram = lax.optimization_barrier((final, gram))
     whole_block = lax.all_gather(final, "vecs", axis=1, tiled=True)
-    panel = lax.dot_general(
-        final, whole_block, (((0,), (0,)), ((), ())), preferred_element_type=jnp.float32
-    )
-    summed = lax.psum(panel_part(panel), "rows")
-    gram = lax.all_gather(summed, "vecs", axis=0, tiled=True)
-    inverse = inverse_factor(gram, total_rows, lax.axis_size("vecs"))
+    inverse = inverse_factor(gram, total_rows)
     own_rows = lax.dynamic_slice_in_dim(
         inverse, lax.axis_index("vecs") * panel_width, panel_width, 0
     )

time: 382 us -> 291 us (0.76)
  waiting for transfers between devices: 194 us -> 0.02 us
  Pallas kernels: 148 us -> 261 us
  matrix products: 21.8 us -> 12.2 us
    pallas_call x1 -> x2, Pallas kernels: 65.6 us -> 179 us  [the longest x1 113 us: gram_sum(): pl.pallas_call(functools.partial(gram_kernel, stages), out_shape=jax.Shap...]
    all_gather x1, waiting for transfers between devices: 94 us -> 0.01 us  [shards(): whole_block = lax.all_gather(final, 'vecs', axis=1, tiled=True)]
    psum x1 -> x0, waiting for transfers between devices: 72.9 us -> none  [shards(): summed = lax.psum(panel_part(panel), 'rows')]
    all_gather x1 -> x0, waiting for transfers between devices: 27.1 us -> none  [shards(): gram = lax.all_gather(summed, 'vecs', axis=0, tiled=True)]
    dot_general x1 -> x0, matrix products: 7.37 us -> none  [shards(): lax.dot_general(final, whole_block, (((0,), (0,)), ((), ())), preferred_e...]
  transfers between devices with their start and end apart: 3 -> 1, of which waited for: 3 -> 0; matrix products, arithmetic and copies ran while one was open for 0% -> 0% of each run, Pallas kernels for 0% -> 23%
where the time goes in v2:
time: 291 us; the launch traced here: 288 us
  Pallas kernels  261 us (90%)
  between operations  13.4 us (5%)
  matrix products  12.2 us (4%)
    pallas_call x1, Pallas kernels, gram_sum(): pl.pallas_call(functools.partial(gram_kernel, stages), out_shape=jax.Shap...  113 us
    pallas_call x1, Pallas kernels, filtered_block(): pl.pallas_call(filter_kernel, out_shape=jax.ShapeDtypeStruct((block_rows,...  82 us
    pallas_call x1, Pallas kernels, inverse_factor(): pl.pallas_call(functools.partial(inverse_kernel, size, total_rows), out_s...  65.4 us
    dot_general x1, matrix products, split_apply(): first = jnp.dot(left_bf, factor_high.T, preferred_element_type=jnp.float32)  6.24 us
    dot_general x1, matrix products, split_apply(): second = jnp.dot(left_bf, factor_low.T, preferred_element_type=jnp.float32)  5.92 us
  transfers between devices with their start and end apart: 1, of which 0 were waited for; matrix products, arithmetic and copies ran while one was open for 0% of the time, Pallas kernels for 23%

profile of v2, /device:TPU:3, one launch (start us, length us, event | category | flops | bytes accessed | tf_op | source)
XLA Modules:
  0.0 287.7 jit_solution(3919948953627052157)
XLA Ops:
  6.5 0.0 all-gather.2.cloned.1.call-start
  6.6 0.8 copy.5
  7.3 0.7 select_add_fusion.place_ref
  8.0 82.0 %shard_map.37 = bf16[32,128,256]{2,1,0:T(8,128)(2,1)} custom-call(s32[32,5]{1,0:T(8,128)} %select_add_fusion.place_ref, bf16[32,128,256]{2,1,0:T(8,128)(2,1)} %bitcast.6, bf16[32,5,128,128]{3,2,1,0:T(8,128)(2,1)} %blocks_ref.1), custom_call_target="tpu_custom_call" | custom-call | tf_op jit(solution)/shard_map/pallas_call | solution.py:169
  90.0 113.1 %shard_map.38.gram_ref = f32[4,640,256]{2,1,0:T(8,128)} custom-call(bf16[4096,256]{1,0:T(8,128)(2,1)} %bitcast.4), custom_call_target="tpu_custom_call" | custom-call | tf_op jit(solution)/shard_map/pallas_call | solution.py:456
  203.1 0.0 all-gather.2.cloned.1.call-update
  203.2 65.4 %shard_map.39 = f32[1024,1024]{1,0:T(8,128)} custom-call(f32[4,640,256]{2,1,0:T(8,128)} %shard_map.38.gram_ref), custom_call_target="tpu_custom_call" | custom-call | flops 42949672960 | bytes 8388608 | tf_op jit(solution)/shard_map/pallas_call | solution.py:541
  268.6 0.0 all-gather.2.cloned.1.call-done
  268.6 0.0 copy-start
  268.6 6.2 %fusion = f32[4096,256]{1,0:T(8,128)S(1)} fusion(bf16[4096,1024]{1,0:T(8,128)(2,1)} %all-gather.2.cloned.1.call-done, f32[1024,1024]{1,0:T(8,128)} %shard_map.39, s32[]{:T(128)S(6)} %select_n.14), kind=kOutput, calls=%fused_computation.3 | convolution fusion | flops 2147483648 | bytes 13107204 | tf_op jit(solution)/shard_map/dot_general | solution.py:560
  274.9 0.0 copy-done
  274.9 5.9 %convolution_add_fusion = f32[4096,256]{1,0:T(8,128)} fusion(f32[4096,256]{1,0:T(8,128)S(1)} %fusion, bf16[4096,1024]{1,0:T(8,128)(2,1)S(1)} %copy-done, f32[1024,1024]{1,0:T(8,128)} %shard_map.39, s32[]{:T(128)S(6)} %select_n.14), kind=kOutput, calls=%fused_computation | convolution fusion | flops 2149580800 | bytes 17825796 | tf_op jit(solution)/shard_map/dot_general | solution.py:561
  (2 shorter events, 0.0 us)
Async XLA Ops:
  6.5 262.1 %all-gather.2.cloned.1.call-start = ((), (), s32[]{:S(2)}) async-start(), calls=%async_computation | async-start | bytes 10485760 | tf_op jit(solution)/shard_map/all_gather | solution.py:571
  268.6 6.3 %copy-start = (bf16[4096,1024]{1,0:T(8,128)(2,1)S(1)}, bf16[4096,1024]{1,0:T(8,128)(2,1)}, u32[]{:S(2)}) copy-start(bf16[4096,1024]{1,0:T(8,128)(2,1)} %all-gather.2.cloned.1.call-done) | copy-start | bytes 25165828
Sparse Core Ops, SparseCore 0:
  203.3 59.4 all-gather.1
